TPU v7x, 256 devices: a whole 4x4x8 slice. The times are simulated.
256 devices in a mesh: fac: 4 (over y_lo, core), col: 64 (over y_hi, x, z).
Axes of the slice: x: 4, y: 4 (y_hi: 2, y_lo: 2; y = y_hi * 2 + y_lo), z: 8, core: 2. Of those that a mesh axis runs over, the one named last changes fastest.
Arguments:
- lower_factor: bfloat16 [1, 4, 4, 256, 256], P(None, 'fac', None, None, 'col'), may hold values from -0.1875 to 0.1875
- panel_inverse: float32 [1, 4, 256, 256], P(None, 'fac', None, 'col'), may hold values from -0.375 to 0.375
- right_side: float32 [1, 4, 256, 8192], P(None, 'fac', None, 'col'), may hold values from -0.1875 to 0.1875
- fill: int32 [4, 4], replicated, may hold values 0 or 1
Outputs:
- schur: float32 [8192, 4, 2048], P('col', 'fac')
All inputs are finite; a program needn't handle non-finite values.
Results may differ from a plain program's by a relative error of at most 0.0034.
Values may be sent and summed in bfloat16 or wider, within the bound.
No kernel may reach another device: no remote copies, remote signals or barrier semaphores. Data moves between devices by JAX's collectives and lax.ppermute only.
A program may use at most 64 MiB of HBM per device.

v0:
```python
import jax
import jax.numpy as jnp
from jax import lax
from jax.sharding import PartitionSpec as P


def broadcast(array, axis, root):
    mine = lax.axis_index(axis) == root
    return lax.psum(jnp.where(mine, array, jnp.zeros_like(array)), axis)


def per_device(lower_factor, panel_inverse, right_side, fill):
    panels = lower_factor.shape[0]
    fac_count = lax.axis_size("fac")
    my_index = lax.axis_index("fac")
    inverses = lax.all_gather(panel_inverse, "col", axis=3, tiled=True)[:, 0]
    pending = right_side[:, 0]
    solved = jnp.zeros(pending.shape, jnp.bfloat16)
    total_panels = panels * fac_count
    selector = (jnp.arange(fac_count) == my_index).astype(jnp.int32)
    for owner in range(fac_count):
        own_solve = jnp.dot(
            inverses[0],
            pending[0],
            precision=lax.Precision.HIGHEST,
            preferred_element_type=jnp.float32,
        ).astype(jnp.bfloat16)
        panel_rows = broadcast(own_solve, "fac", owner)
        solved = solved.at[0].set(jnp.where(my_index == owner, panel_rows, solved[0]))
        if owner + 1 < total_panels:
            later_blocks = lower_factor[0:, 0, owner]
            column_flags = fill[:, owner].reshape(panels, fac_count)
            flags = jnp.sum(column_flags * selector[None, :], axis=1)
            targets = jnp.arange(0, panels) * fac_count + my_index
            keep_mask = ((flags == 1) & (targets > owner)).astype(jnp.float32)
            update = jnp.einsum(
                "nab,bm->nam",
                lax.all_gather(later_blocks, "col", axis=2, tiled=True),
                panel_rows,
                preferred_element_type=jnp.float32,
            )
            pending = pending.at[0:].add(-keep_mask[:, None, None] * update)
    slab_flat = solved.reshape(-1, solved.shape[2])
    columns_dev = slab_flat.shape[1]
    share = columns_dev // fac_count
    all_rows = lax.all_gather(slab_flat, "fac", axis=0, tiled=True)
    my_share = lax.dynamic_slice_in_dim(all_rows, my_index * share, share, 1)
    products = lax.dot_general(
        all_rows,
        lax.all_gather(my_share, "col", axis=1, tiled=True),
        (((0,), (0,)), ((), ())),
        preferred_element_type=jnp.float32,
    )
    result = products[:, None, :]
    return result


def solution(mesh):
    return jax.shard_map(
        per_device,
        mesh=mesh,
        in_specs=(
            P(None, "fac", None, None, "col"),
            P(None, "fac", None, "col"),
            P(None, "fac", None, "col"),
            P(),
        ),
        out_specs=P("col", "fac", None),
        check_vma=False,
    )
```

profile of v0, /device:TPU:2, one launch (start us, length us, event | category | flops | bytes accessed | tf_op | source)
XLA Modules:
  0.0 919.4 jit_solution(4776379949293501510)
XLA Ops:
  6.5 0.0 all-reduce.5.cloned.1.call-start
  6.5 0.7 copy.21
  7.2 164.2 %all_gather.18 = f32[1,1,256,256]{2,1,0,3:T(1,128)S(1)} all-gather(f32[1,1,256,4]{2,1,0,3:T(1,128)S(1)} %copy.21), channel_id=1, replica_groups=mesh['fac'=4,'col'=64] {'col'}, dimensions={3}, use_global_device_ids=true | all-gather | bytes 266240 | tf_op jit(solution)/shard_map/all_gather | solution.py:16
  171.4 2.1 fusion.6
  173.6 0.0 all-reduce.5.cloned.1.call-update
  173.6 0.0 all-reduce.7.cloned.1.call-start
  173.6 1.0 slice_reduce_fusion
  174.6 0.7 fusion.28
  175.4 0.7 fusion.27
  176.0 1.0 copy.20
  177.7 175.3 %all-gather = bf16[1,1,1,256,256]{3,2,1,0,4:T(2,128)(2,1)S(1)} all-gather(bf16[1,1,1,256,4]{3,2,1,0,4:T(2,128)(2,1)S(1)} %copy.37), channel_id=2, replica_groups=mesh['fac'=4,'col'=64] {'col'}, dimensions={4}, use_global_device_ids=true | all-gather | bytes 133120 | tf_op jit(solution)/shard_map/all_gather | solution.py:38
  353.0 0.1 copy.23
  353.1 0.0 all-reduce.5.cloned.1.call-done
  353.2 0.0 copy-start
  353.2 1.1 fusion.3
  354.3 1.2 fusion.8
  355.5 0.0 all-reduce.7.cloned.1.call-update
  355.5 0.0 all-reduce.9.cloned.1.call-start
  355.6 0.6 fusion.26
  356.8 177.2 %all-gather.1 = bf16[1,1,1,256,256]{3,2,1,0,4:T(2,128)(2,1)S(1)} all-gather(bf16[1,1,1,256,4]{3,2,1,0,4:T(2,128)(2,1)S(1)} %copy.38), channel_id=3, replica_groups=mesh['fac'=4,'col'=64] {'col'}, dimensions={4}, use_global_device_ids=true | all-gather | bytes 133120 | tf_op jit(solution)/shard_map/all_gather | solution.py:38
  534.0 0.1 copy.26
  534.2 0.0 all-reduce.7.cloned.1.call-done
  534.2 1.0 fusion.4
  535.2 1.2 fusion.10
  536.5 0.0 all-reduce.9.cloned.1.call-update
  536.5 0.0 all-reduce.11.cloned.1.call-start
  536.5 0.7 fusion.25
  537.9 175.4 %all-gather.2 = bf16[1,1,1,256,256]{3,2,1,0,4:T(2,128)(2,1)S(1)} all-gather(bf16[1,1,1,256,4]{3,2,1,0,4:T(2,128)(2,1)S(1)} %copy.39), channel_id=4, replica_groups=mesh['fac'=4,'col'=64] {'col'}, dimensions={4}, use_global_device_ids=true | all-gather | bytes 133120 | tf_op jit(solution)/shard_map/all_gather | solution.py:38
  713.3 0.1 copy.29
  713.4 0.0 all-reduce.9.cloned.1.call-done
  713.4 1.0 fusion.5
  714.5 1.2 fusion.12
  715.7 0.0 all-reduce.11.cloned.1.call-update
  715.7 0.0 all-gather.5.cloned.1.call-start
  715.8 55.5 %all-reduce.11.cloned.1.call-done = bf16[256,128]{1,0:T(8,128)(2,1)} async-done(((bf16[256,128]{1,0:T(8,128)(2,1)}), bf16[256,128]{1,0:T(8,128)(2,1)}) %all-reduce.11.cloned.1.call-update) | async-done | bytes 65552 | tf_op jit(solution)/shard_map/psum | solution.py:9
  771.3 0.0 copy-done
  771.3 6.2 all_gather.22
  777.5 0.1 constant_dynamic-slice_fusion
  777.7 0.8 copy.31
  778.4 0.0 all-gather.5.cloned.1.call-update
  778.5 128.6 %all-gather.5.cloned.1.call-done = bf16[1024,2048]{0,1:T(8,128)(2,1)} async-done(((bf16[1024,32]{0,1:T(8,128)(2,1)}), bf16[1024,2048]{0,1:T(8,128)(2,1)}) %all-gather.5.cloned.1.call-update) | async-done | bytes 4194320 | tf_op jit(solution)/shard_map/all_gather | solution.py:50
  907.1 3.7 convolution_bitcast_fusion
  910.8 2.0 copy.32
  (4 shorter events, 0.0 us)
Async XLA Ops:
  6.5 346.6 %all-reduce.5.cloned.1.call-start = ((), (), s32[]{:S(2)}) async-start(), calls=%async_computation | async-start | bytes 131072 | tf_op jit(solution)/shard_map/psum | solution.py:9
  173.6 360.6 %all-reduce.7.cloned.1.call-start = ((), (), s32[]{:S(2)}) async-start(), calls=%async_computation.1 | async-start | bytes 131072 | tf_op jit(solution)/shard_map/psum | solution.py:9
  353.2 418.1 %copy-start = (bf16[256,128]{1,0:T(8,128)(2,1)S(1)}, bf16[256,128]{1,0:T(8,128)(2,1)}, u32[]{:S(2)}) copy-start(bf16[256,128]{1,0:T(8,128)(2,1)} %all-reduce.5.cloned.1.call-done) | copy-start | bytes 196612
  355.5 357.9 %all-reduce.9.cloned.1.call-start = ((), (), s32[]{:S(2)}) async-start(), calls=%async_computation.2 | async-start | bytes 131072 | tf_op jit(solution)/shard_map/psum | solution.py:9
  536.5 234.8 %all-reduce.11.cloned.1.call-start = ((), (), s32[]{:S(2)}) async-start(), calls=%async_computation.3 | async-start | bytes 131072 | tf_op jit(solution)/shard_map/psum | solution.py:9
  715.7 191.3 %all-gather.5.cloned.1.call-start = ((), (), s32[]{:S(2)}) async-start(), calls=%async_computation.4 | async-start | bytes 4259840 | tf_op jit(solution)/shard_map/all_gather | solution.py:50
Sparse Core Ops, SparseCore 0:
  173.7 54.0 all-reduce.4
  355.7 55.3 all-reduce.6
  536.6 54.0 all-reduce.8
  715.9 55.3 all-reduce.10
  778.6 128.4 all-gather.4
where the time goes:
time: 920 us; the launch traced here: 919 us
  blocking collectives  698 us (76%)
  waiting for transfers between devices  184 us (20%)
  between operations  15.1 us (2%)
  matrix products  12.7 us (1%)
    all_gather x3, blocking collectives, per_device(): lax.all_gather(later_blocks, 'col', axis=2, tiled=True)  528 us
    all_gather x1, blocking collectives, per_device(): inverses = lax.all_gather(panel_inverse, 'col', axis=3, tiled=True)[:, 0]  164 us
    all_gather x1, waiting for transfers between devices, per_device(): lax.all_gather(my_share, 'col', axis=1, tiled=True)  129 us
    psum x4, waiting for transfers between devices, broadcast(): return lax.psum(jnp.where(mine, array, jnp.zeros_like(array)), axis)  55.5 us
  transfers between devices with their start and end apart: 5, of which 2 were waited for; matrix products, arithmetic and copies ran while one was open for 1% of the time, Pallas kernels for 0%

commit v1 on v0

--- a/solution.py
+++ b/solution.py
@@ -35,7 +35,10 @@
             keep_mask = ((flags == 1) & (targets > owner)).astype(jnp.float32)
             update = jnp.einsum(
                 "nab,bm->nam",
-                lax.all_gather(later_blocks, "col", axis=2, tiled=True),
+                jnp.concatenate(
+                    lax.all_to_all(jnp.stack([later_blocks] * lax.axis_size("col")), "col", 0, 0),
+                    axis=2,
+                ),
                 panel_rows,
                 preferred_element_type=jnp.float32,
             )

time: 920 us -> 523 us (0.57)
  blocking collectives: 698 us -> 167 us
  waiting for transfers between devices: 184 us -> 262 us
  starting transfers between devices: 0.17 us -> 53.9 us
    all_gather x3 -> x0, blocking collectives: 528 us -> none  [per_device(): lax.all_gather(later_blocks, 'col', axis=2, tiled=True)]
    psum x4, waiting for transfers between devices: 55.5 us -> 133 us  [broadcast(): return lax.psum(jnp.where(mine, array, jnp.zeros_like(array)), axis)]
    all_to_all x0 -> x3, starting transfers between devices: none -> 53.7 us  [per_device(): lax.all_to_all(jnp.stack([later_blocks] * lax.axis_size('col')), 'col', 0...]
  transfers between devices with their start and end apart: 5 -> 8, of which waited for: 2 -> 5; matrix products, arithmetic and copies ran while one was open for 1% -> 2% of each run, Pallas kernels for 0% -> 0%
where the time goes in v1:
time: 523 us; the launch traced here: 522 us
  waiting for transfers between devices  262 us (50%)
  blocking collectives  167 us (32%)
  starting transfers between devices  53.9 us (10%)
  between operations  15.1 us (3%)
  matrix products  12.6 us (2%)
  local copies, waits for them, and re-layouts  8.54 us (2%)
    all_gather x1, blocking collectives, per_device(): inverses = lax.all_gather(panel_inverse, 'col', axis=3, tiled=True)[:, 0]  161 us
    psum x4, waiting for transfers between devices, broadcast(): return lax.psum(jnp.where(mine, array, jnp.zeros_like(array)), axis)  133 us
    all_gather x1, waiting for transfers between devices, per_device(): lax.all_gather(my_share, 'col', axis=1, tiled=True)  129 us
    all_to_all x3, starting transfers between devices, per_device(): lax.all_to_all(jnp.stack([later_blocks] * lax.axis_size('col')), 'col', 0...  53.7 us
  transfers between devices with their start and end apart: 8, of which 5 were waited for; matrix products, arithmetic and copies ran while one was open for 2% of the time, Pallas kernels for 0%

profile of v1, /device:TPU:2, one launch (start us, length us, event | category | flops | bytes accessed | tf_op | source)
XLA Modules:
  0.0 522.1 jit_solution(3908540455276330916)
XLA Ops:
  6.5 0.7 slice_bitcast_fusion
  7.3 0.7 stack.9
  7.9 14.6 %all-to-all-start = ((bf16[64,1,256,4]{2,3,1,0:T(4,128)(2,1)}), bf16[64,1,256,4]{2,3,1,0:T(4,128)(2,1)S(1)}, u32[]{:S(2)}, u32[]{:S(2)}) async-start(bf16[64,1,256,4]{2,3,1,0:T(4,128)(2,1)} %stack.9), calls=%async_computation | async-start | bytes 262144 | tf_op jit(solution)/shard_map/all_to_all | solution.py:39
  22.6 0.0 all-reduce.5.cloned.1.call-start
  22.7 0.7 copy.19
  23.4 161.1 %all_gather.9 = f32[1,1,256,256]{2,1,0,3:T(1,128)S(1)} all-gather(f32[1,1,256,4]{2,1,0,3:T(1,128)S(1)} %copy.19), channel_id=1, replica_groups=mesh['fac'=4,'col'=64] {'col'}, dimensions={3}, use_global_device_ids=true | all-gather | bytes 266240 | tf_op jit(solution)/shard_map/all_gather | solution.py:16
  184.4 2.1 fusion.6
  186.5 0.0 all-reduce.5.cloned.1.call-update
  186.6 1.0 copy.18
  187.6 1.0 slice_reduce_fusion
  188.6 0.6 fusion.24
  189.8 0.0 all-to-all-done
  189.8 0.7 stack.10
  190.5 26.4 %all-to-all-start.1 = ((bf16[64,1,256,4]{2,3,1,0:T(4,128)(2,1)}), bf16[64,1,256,4]{2,3,1,0:T(4,128)(2,1)S(1)}, u32[]{:S(2)}, u32[]{:S(2)}) async-start(bf16[64,1,256,4]{2,3,1,0:T(4,128)(2,1)} %stack.10), calls=%async_computation.1 | async-start | bytes 262144 | tf_op jit(solution)/shard_map/all_to_all | solution.py:39
  216.9 0.0 all-reduce.7.cloned.1.call-start
  217.0 23.5 %all-reduce.5.cloned.1.call-done = bf16[256,128]{1,0:T(8,128)(2,1)} async-done(((bf16[256,128]{1,0:T(8,128)(2,1)}), bf16[256,128]{1,0:T(8,128)(2,1)}) %all-reduce.5.cloned.1.call-update) | async-done | bytes 65552 | tf_op jit(solution)/shard_map/psum | solution.py:9
  240.4 1.0 fusion.3
  241.5 1.2 fusion.8
  242.7 0.0 all-reduce.7.cloned.1.call-update
  242.7 0.7 fusion.23
  244.0 0.0 all-to-all-done.1
  244.1 0.7 stack.11
  244.7 12.7 %all-to-all-start.2 = ((bf16[64,1,256,4]{2,3,1,0:T(4,128)(2,1)}), bf16[64,1,256,4]{2,3,1,0:T(4,128)(2,1)S(1)}, u32[]{:S(2)}, u32[]{:S(2)}) async-start(bf16[64,1,256,4]{2,3,1,0:T(4,128)(2,1)} %stack.11), calls=%async_computation.2 | async-start | bytes 262144 | tf_op jit(solution)/shard_map/all_to_all | solution.py:39
  257.4 0.0 all-reduce.9.cloned.1.call-start
  257.5 27.6 %all-reduce.7.cloned.1.call-done = bf16[256,128]{1,0:T(8,128)(2,1)} async-done(((bf16[256,128]{1,0:T(8,128)(2,1)}), bf16[256,128]{1,0:T(8,128)(2,1)}) %all-reduce.7.cloned.1.call-update) | async-done | bytes 65552 | tf_op jit(solution)/shard_map/psum | solution.py:9
  285.1 1.0 fusion.4
  286.1 1.2 fusion.10
  287.4 0.0 all-reduce.9.cloned.1.call-update
  287.4 0.0 all-reduce.11.cloned.1.call-start
  287.4 0.7 fusion.22
  288.8 0.0 all-to-all-done.2
  288.8 40.6 %all-reduce.9.cloned.1.call-done = bf16[256,128]{1,0:T(8,128)(2,1)} async-done(((bf16[256,128]{1,0:T(8,128)(2,1)}), bf16[256,128]{1,0:T(8,128)(2,1)}) %all-reduce.9.cloned.1.call-update) | async-done | bytes 65552 | tf_op jit(solution)/shard_map/psum | solution.py:9
  329.4 1.0 fusion.5
  330.4 1.2 fusion.12
  331.6 0.0 all-reduce.11.cloned.1.call-update
  331.7 0.0 all-gather.2.cloned.1.call-start
  331.7 41.8 %all-reduce.11.cloned.1.call-done = bf16[256,128]{1,0:T(8,128)(2,1)} async-done(((bf16[256,128]{1,0:T(8,128)(2,1)}), bf16[256,128]{1,0:T(8,128)(2,1)}) %all-reduce.11.cloned.1.call-update) | async-done | bytes 65552 | tf_op jit(solution)/shard_map/psum | solution.py:9
  373.5 0.9 select_select_fusion
  374.3 5.9 %all_gather.10 = bf16[1024,128]{1,0:T(8,128)(2,1)S(1)} all-gather(bf16[256,128]{1,0:T(8,128)(2,1)S(1)} %select_select_fusion), channel_id=1, replica_groups=mesh['fac'=4,'col'=64] {'fac'}, dimensions={0}, use_global_device_ids=true | all-gather | bytes 327680 | tf_op jit(solution)/shard_map/all_gather | solution.py:49
  380.2 0.1 constant_dynamic-slice_fusion
  380.4 0.8 copy.23
  381.1 0.0 all-gather.2.cloned.1.call-update
  381.1 128.6 %all-gather.2.cloned.1.call-done = bf16[1024,2048]{0,1:T(8,128)(2,1)} async-done(((bf16[1024,32]{0,1:T(8,128)(2,1)}), bf16[1024,2048]{0,1:T(8,128)(2,1)}) %all-gather.2.cloned.1.call-update) | async-done | bytes 4194320 | tf_op jit(solution)/shard_map/all_gather | solution.py:53
  509.8 3.7 convolution_bitcast_fusion
  513.5 2.0 copy.24
  (3 shorter events, 0.1 us)
Async XLA Ops:
  7.9 181.9 %all-to-all-start = ((bf16[64,1,256,4]{2,3,1,0:T(4,128)(2,1)}), bf16[64,1,256,4]{2,3,1,0:T(4,128)(2,1)S(1)}, u32[]{:S(2)}, u32[]{:S(2)}) async-start(bf16[64,1,256,4]{2,3,1,0:T(4,128)(2,1)} %stack.9), calls=%async_computation | async-start | bytes 262144 | tf_op jit(solution)/shard_map/all_to_all | solution.py:39
  22.6 217.8 %all-reduce.5.cloned.1.call-start = ((), (), s32[]{:S(2)}) async-start(), calls=%async_computation.3 | async-start | bytes 131072 | tf_op jit(solution)/shard_map/psum | solution.py:9
  190.5 53.5 %all-to-all-start.1 = ((bf16[64,1,256,4]{2,3,1,0:T(4,128)(2,1)}), bf16[64,1,256,4]{2,3,1,0:T(4,128)(2,1)S(1)}, u32[]{:S(2)}, u32[]{:S(2)}) async-start(bf16[64,1,256,4]{2,3,1,0:T(4,128)(2,1)} %stack.10), calls=%async_computation.1 | async-start | bytes 262144 | tf_op jit(solution)/shard_map/all_to_all | solution.py:39
  216.9 68.2 %all-reduce.7.cloned.1.call-start = ((), (), s32[]{:S(2)}) async-start(), calls=%async_computation.4 | async-start | bytes 131072 | tf_op jit(solution)/shard_map/psum | solution.py:9
  244.7 44.0 %all-to-all-start.2 = ((bf16[64,1,256,4]{2,3,1,0:T(4,128)(2,1)}), bf16[64,1,256,4]{2,3,1,0:T(4,128)(2,1)S(1)}, u32[]{:S(2)}, u32[]{:S(2)}) async-start(bf16[64,1,256,4]{2,3,1,0:T(4,128)(2,1)} %stack.11), calls=%async_computation.2 | async-start | bytes 262144 | tf_op jit(solution)/shard_map/all_to_all | solution.py:39
  257.4 71.9 %all-reduce.9.cloned.1.call-start = ((), (), s32[]{:S(2)}) async-start(), calls=%async_computation.5 | async-start | bytes 131072 | tf_op jit(solution)/shard_map/psum | solution.py:9
  287.4 86.1 %all-reduce.11.cloned.1.call-start = ((), (), s32[]{:S(2)}) async-start(), calls=%async_computation.6 | async-start | bytes 131072 | tf_op jit(solution)/shard_map/psum | solution.py:9
  331.7 178.1 %all-gather.2.cloned.1.call-start = ((), (), s32[]{:S(2)}) async-start(), calls=%async_computation.7 | async-start | bytes 4259840 | tf_op jit(solution)/shard_map/all_gather | solution.py:53
Sparse Core Ops, SparseCore 0:
  186.7 53.7 all-reduce.4
  243.0 42.0 all-reduce.6
  287.7 41.5 all-reduce.8
  331.8 41.5 all-reduce.10
  381.3 128.4 all-gather.1
